TPU v7x, 32 devices: a whole 2x2x4 slice. The times are simulated.
32 devices in a mesh: cuts: 2 (over x), mode: 8 (over z, y), branch: 2 (over core).
Axes of the slice: x: 2, y: 2, z: 4, core: 2. Of those that a mesh axis runs over, the one named last changes fastest.
Arguments:
- leaves: bfloat16 [8, 2, 32, 512, 512], P('branch', None, ('cuts', 'mode')), parts along dimension 2, may hold values from -0.1875 to 0.1875
- join_order: int32 [7], replicated, may hold values from 0 to 1
- slice_values: int32 [32], P(('cuts', 'mode')), parts along dimension 0, may hold values from 0 to 1
- boundary: bfloat16 [2, 2, 512, 512], replicated, may hold values from -4 to 4
Outputs:
- amplitudes: float32 [2, 32, 512, 512], P(None, ('cuts', 'mode'), 'branch'), parts along dimension 1
There are 2 independent parts, one for each index of `cuts`. A program takes and returns all parts, laid end to end along the dimension named above; an argument that names none is the same for every part. Nothing has to cross between parts.
Inputs may be any that keep to these rules, and one draw needn't show every extreme that they name: `join_order`: 1 puts the second operand of the join on the left.
All inputs are finite; a program needn't handle non-finite values.
Results may differ from a plain program's by a relative error of at most 0.0076.
Values may be sent and summed in bfloat16 or wider, within the bound.
A program may use at most 64 MiB of HBM per device.

v0:
```python
import functools

import jax
import jax.numpy as jnp
from jax import lax
from jax.experimental import pallas as pl
from jax.experimental.pallas import tpu as pltpu
from jax.sharding import PartitionSpec as P

MESH = pl.DeviceIdType.MESH


def dot(left, right):
    return jnp.dot(left, right, preferred_element_type=jnp.float32)


def complex_rows(left_real, left_imag, right_real, right_imag):
    real_part = dot(left_real, right_real) - dot(left_imag, right_imag)
    imag_part = dot(left_real, right_imag) + dot(left_imag, right_real)
    return real_part, imag_part


def contract_kernel(
    per, order_ref, leaves_ref, out_ref, prod, right, left, result,
    leaf_sem, own_right, own_left,
    cross_right_send, cross_right_recv, cross_left_send, cross_left_recv,
    column_send, column_recv, relay_send, relay_recv,
    deliver_send, deliver_recv, forward_send, forward_recv, *leaf,
):
    n = lax.axis_size("mode")
    group = n // per
    pair = 2
    peers = group // pair
    rounds = n // pair
    wide = pair * per
    m = lax.axis_index("mode")
    core = lax.axis_index("branch")
    h, g = m // group, lax.rem(m, group)
    line, side = g // pair, lax.rem(g, pair)
    across = pair * line + 1 - side
    blk, width = out_ref.shape[-2:]
    order = n * blk

    def remote(src, dst, send, recv, **device):
        return pltpu.make_async_remote_copy(
            src_ref=src,
            dst_ref=dst,
            send_sem=send,
            recv_sem=recv,
            device_id=device,
            device_id_type=MESH,
        )

    def column(line_at):
        return pair * line_at + side

    def up(k):
        return lax.rem(line + k, peers)

    def down(k):
        return lax.rem(line + peers - k, peers)

    def own_right_copy(q, e):
        return pltpu.make_async_copy(
            prod.at[0, :, e, pair * q + side], right.at[q, :, per * g + e], own_right.at[q, e]
        )

    def own_left_copy(q, e):
        return pltpu.make_async_copy(
            prod.at[1, :, e, pair * q + side], left.at[q, :, per * side + e], own_left.at[q, e]
        )

    def cross_right(q, e, source=None):
        return remote(
            prod.at[0, :, e, pair * q + 1 - side],
            right.at[q, :, per * (g if source is None else source) + e],
            cross_right_send.at[q, e],
            cross_right_recv.at[q, e],
            mode=h * group + across,
        )

    def cross_left(q, e, source=None):
        return remote(
            prod.at[1, :, e, pair * q + 1 - side],
            left.at[q, :, per * (side if source is None else source) + e],
            cross_left_send.at[q, e],
            cross_left_recv.at[q, e],
            mode=h * group + across,
        )

    def column_right(q, e, k, target, source):
        return remote(
            prod.at[0, :, e, pair * q + side],
            right.at[q, :, per * column(source) + e],
            column_send.at[q, e, k],
            column_recv.at[q, e, k],
            mode=h * group + column(target),
        )

    def relay_right(q, e, k, target, source):
        part = right.at[q, :, per * (pair * source + 1 - side) + e]
        return remote(
            part,
            part,
            relay_send.at[q, e, k],
            relay_recv.at[q, e, k],
            mode=h * group + column(target),
        )

    def spot(q, h_from, side_from):
        batch = per * (pair * q + side_from) + h_from
        return batch // n, lax.rem(batch, n)

    def deliver(q, i):
        entry, row = spot(q, h, side)
        at = pair * h + side
        return remote(
            result.at[q, :, i],
            out_ref.at[core, entry, :, row],
            deliver_send.at[q, i],
            deliver_recv.at[q, at],
            mode=wide * line + i,
        )

    def deliver_own(q, i):
        entry, row = spot(q, h, side)
        return pltpu.make_async_copy(
            result.at[q, :, i],
            out_ref.at[core, entry, :, row],
            deliver_recv.at[q, pair * h + side],
        )

    def delivered(q, h_from, side_from):
        entry, row = spot(q, h_from, side_from)
        part = out_ref.at[core, entry, :, row]
        return pltpu.make_async_copy(part, part, deliver_recv.at[q, pair * h_from + side_from])

    def forward(q, h_from, side_from, owner):
        entry, row = spot(q, h_from, side_from)
        part = out_ref.at[owner, entry, :, row]
        at = pair * h_from + side_from
        return remote(
            part, part, forward_send.at[q, at], forward_recv.at[q, at], branch=1 - core
        )

    def leaf_copy(e):
        return pltpu.make_async_copy(leaves_ref.at[:, :, e], leaf[e], leaf_sem.at[e])

    middle_order = order_ref[4 + core]
    tile = min(256, order)

    def first_join(slot, e):
        which = 1 - middle_order if slot == 0 else middle_order
        flag = order_ref[2 * core + which]
        left_leaf = 2 * which + flag
        right_leaf = 2 * which + 1 - flag

        @pl.loop(0, order // tile)
        def _(step):
            at = pl.ds(pl.multiple_of(step * tile, tile), tile)
            real_part, imag_part = complex_rows(
                leaf[e][left_leaf, 0, at, :],
                leaf[e][left_leaf, 1, at, :],
                leaf[e][right_leaf, 0],
                leaf[e][right_leaf, 1],
            )
            blocks = tile // blk
            shape = (blocks, blk, width)
            to = pl.ds(step * blocks, blocks)
            prod[slot, 0, e, to] = real_part.astype(prod.dtype).reshape(shape)
            prod[slot, 1, e, to] = imag_part.astype(prod.dtype).reshape(shape)

    def send_cross_right(q, e):
        cross_right(q, e).start()

    def send_column(q, e):
        for k in range(1, peers):
            column_right(q, e, k, up(k), line).start()
        own_right_copy(q, e).start()

    def send_cross_left(q, e):
        cross_left(q, e).start()
        own_left_copy(q, e).start()

    def send_relay(q, e):
        cross_right(q, e, across).wait_recv()
        for k in range(1, peers):
            relay_right(q, e, k, up(k), line).start()

    barrier = pltpu.get_barrier_semaphore()
    for k in range(1, n):
        pl.semaphore_signal(
            barrier, inc=1, device_id={"mode": lax.rem(m + k, n)}, device_id_type=MESH
        )
    pl.semaphore_signal(barrier, inc=1, device_id={"branch": 1 - core}, device_id_type=MESH)
    for e in range(per):
        leaf_copy(e).start()

    for e in range(per):
        leaf_copy(e).wait()
        first_join(0, e)
        if e == 0:
            pl.semaphore_wait(barrier, n)
        send_cross_right(0, e)
        send_column(0, e)
    for e in range(per):
        first_join(1, e)
        send_cross_left(0, e)
        send_relay(0, e)
    for q in range(1, rounds):
        for e in range(per):
            send_cross_right(q, e)
        for e in range(per):
            send_cross_left(q, e)

    row_tile = wide * blk
    for q in range(rounds):
        if q + 1 < rounds:
            for e in range(per):
                send_column(q + 1, e)
        for e in range(per):
            own_right_copy(q, e).wait()
            own_left_copy(q, e).wait()
            cross_left(q, e, 1 - side).wait_recv()
            for k in range(1, peers):
                column_right(q, e, k, down(k), down(k)).wait_recv()
                relay_right(q, e, k, down(k), down(k)).wait_recv()

        real_part, imag_part = complex_rows(
            left[q, 0].reshape(row_tile, width),
            left[q, 1].reshape(row_tile, width),
            right[q, 0].reshape(order, width),
            right[q, 1].reshape(order, width),
        )
        result[q, 0] = real_part.astype(result.dtype).reshape(wide, blk, width)
        result[q, 1] = imag_part.astype(result.dtype).reshape(wide, blk, width)

        for i in range(wide):
            here = wide * line + i == m

            @pl.when(jnp.logical_not(here))
            def _():
                deliver(q, i).start()

            @pl.when(here)
            def _():
                deliver_own(q, i).start()

        if q + 1 < rounds:
            for e in range(per):
                send_relay(q + 1, e)

    for q in range(rounds):
        for h_from in range(per):
            for side_from in range(pair):
                delivered(q, h_from, side_from).wait()
                forward(q, h_from, side_from, core).start()

    for q in range(rounds):
        for e in range(per):
            cross_right(q, e).wait_send()
            cross_left(q, e).wait_send()
            for k in range(1, peers):
                column_right(q, e, k, up(k), line).wait_send()
                relay_right(q, e, k, up(k), line).wait_send()
        for i in range(wide):

            @pl.when(wide * line + i != m)
            def _():
                deliver(q, i).wait_send()

        for h_from in range(per):
            for side_from in range(pair):
                forward(q, h_from, side_from, core).wait_send()
                forward(q, h_from, side_from, 1 - core).wait_recv()


def lower_levels(leaves, join_order):
    n = lax.axis_size("mode")
    count, _, per, order, width = leaves.shape
    blk = order // n
    rounds, peers, wide = n // 2, n // per // 2, 2 * per
    dma = pltpu.SemaphoreType.DMA
    dtype = leaves.dtype
    return pl.pallas_call(
        functools.partial(contract_kernel, per),
        out_shape=jax.ShapeDtypeStruct((2, per, 2, n, blk, width), dtype),
        in_specs=[
            pl.BlockSpec(memory_space=pltpu.SMEM),
            pl.BlockSpec(memory_space=pl.ANY),
        ],
        out_specs=pl.BlockSpec(memory_space=pl.ANY),
        scratch_shapes=[
            pltpu.VMEM((2, 2, per, n, blk, width), dtype),
            pltpu.VMEM((rounds, 2, n, blk, width), dtype),
            pltpu.VMEM((rounds, 2, wide, blk, width), dtype),
            pltpu.VMEM((rounds, 2, wide, blk, width), dtype),
            dma((per,)),
            dma((rounds, per)),
            dma((rounds, per)),
            dma((rounds, per)),
            dma((rounds, per)),
            dma((rounds, per)),
            dma((rounds, per)),
            dma((rounds, per, peers)),
            dma((rounds, per, peers)),
            dma((rounds, per, peers)),
            dma((rounds, per, peers)),
            dma((rounds, wide)),
            dma((rounds, wide)),
            dma((rounds, wide)),
            dma((rounds, wide)),
        ]
        + [pltpu.VMEM((count, 2, order, width), dtype)] * per,
        compiler_params=pltpu.CompilerParams(collective_id=0, has_side_effects=True),
        name="lower_levels",
    )(join_order, leaves)


def top_kernel(order_ref, slices_ref, left_ref, right_ref, chosen_ref, out_ref):
    half = out_ref.shape[-2]
    at = pl.ds(pl.multiple_of(lax.axis_index("branch") * half, half), half)
    top_real, top_imag = complex_rows(
        left_ref[0, 0, 0, at, :], left_ref[0, 0, 1, at, :], right_ref[0, 0, 0], right_ref[0, 0, 1]
    )
    dtype = left_ref.dtype
    real_part, imag_part = complex_rows(
        top_real.astype(dtype), top_imag.astype(dtype), chosen_ref[0, 0], chosen_ref[0, 1]
    )
    out_ref[0, 0] = real_part
    out_ref[1, 0] = imag_part


def top_join(middles, boundary, join_order, slice_values, per):
    order, width = boundary.shape[-2:]
    half = order // 2
    last = join_order.shape[0] - 1
    return pl.pallas_call(
        top_kernel,
        out_shape=jax.ShapeDtypeStruct((2, per, half, width), jnp.float32),
        grid_spec=pltpu.PrefetchScalarGridSpec(
            num_scalar_prefetch=2,
            grid=(per,),
            in_specs=[
                pl.BlockSpec((1, 1, 2, order, width), lambda e, o, s: (o[last], e, 0, 0, 0)),
                pl.BlockSpec((1, 1, 2, order, width), lambda e, o, s: (1 - o[last], e, 0, 0, 0)),
                pl.BlockSpec((1, 2, order, width), lambda e, o, s: (s[e], 0, 0, 0)),
            ],
            out_specs=pl.BlockSpec((2, 1, half, width), lambda e, o, s: (0, e, 0, 0)),
        ),
        name="top_join",
    )(join_order, slice_values, middles, middles, boundary)


def per_device(leaves, join_order, slice_values, boundary):
    _, _, per, order, width = leaves.shape
    middles = lower_levels(leaves, join_order).reshape(2, per, 2, order, width)
    return top_join(middles, boundary, join_order, slice_values, per)


def solution(mesh):
    in_specs = (P("branch", None, ("cuts", "mode"), None, None), P(), P(("cuts", "mode")), P())
    out_specs = P(None, ("cuts", "mode"), "branch", None)
    return jax.shard_map(
        per_device, mesh=mesh, in_specs=in_specs, out_specs=out_specs, check_vma=False
    )
```

profile of v0, /device:TPU:11, one launch (start us, length us, event | category | flops | bytes accessed | tf_op | source)
XLA Modules:
  0.0 91.3 jit_solution(9436951426521113589)
XLA Ops:
  0.0 85.2 %lower_levels.1 = bf16[2,2,2,8,64,512]{5,4,3,2,1,0:T(8,128)(2,1)} custom-call(s32[7]{0:T(128)} %order_ref.3, bf16[4,2,2,512,512]{4,3,2,1,0:T(8,128)(2,1)} %leaves_ref.1), custom_call_target="tpu_custom_call" | custom-call | tf_op jit(solution)/shard_map/lower_levels/pallas_call | solution.py:285
  85.2 6.1 %top_join.1 = f32[2,2,256,512]{3,2,1,0:T(8,128)} custom-call(s32[7]{0:T(128)} %order_ref.3, s32[2]{0:T(128)} %slices_ref.1, bf16[2,2,2,512,512]{4,3,2,1,0:T(8,128)(2,1)} %bitcast.1, bf16[2,2,2,512,512]{4,3,2,1,0:T(8,128)(2,1)} %bitcast.2, bf16[2,2,512,512]{3,2,1,0:T(8,128)(2,1)} %chosen_ref.1), custom_call_target="tpu_custom_call" | custom-call | tf_op jit(solution)/shard_map/top_join/pallas_call | solution.py:338
where the time goes:
time: 92 us; the launch traced here: 91.3 us
  Pallas kernels  91.3 us (99%)
    pallas_call x1, Pallas kernels, lower_levels(): pl.pallas_call(functools.partial(contract_kernel, per), out_shape=jax.Sha...  85.2 us
    pallas_call x1, Pallas kernels, top_join(): pl.pallas_call(top_kernel, out_shape=jax.ShapeDtypeStruct((2, per, half,...  6.08 us

commit v1 on v0

v1 whole, which is shorter than its diff:
```python
import functools

import jax
import jax.numpy as jnp
from jax import lax
from jax.experimental import pallas as pl
from jax.experimental.pallas import tpu as pltpu
from jax.sharding import PartitionSpec as P

MESH = pl.DeviceIdType.MESH


def dot(left, right):
    return jnp.dot(left, right, preferred_element_type=jnp.float32)


def complex_rows(left_real, left_imag, right_real, right_imag):
    real_part = dot(left_real, right_real) - dot(left_imag, right_imag)
    imag_part = dot(left_real, right_imag) + dot(left_imag, right_real)
    return real_part, imag_part


def contract_kernel(
    per, order_ref, slices_ref, leaves_ref, boundary_ref, out_ref,
    prod, right, left, result, chosen,
    leaf_sem, own_right, own_left,
    cross_right_send, cross_right_recv, cross_left_send, cross_left_recv,
    column_send, column_recv, relay_send, relay_recv,
    deliver_send, deliver_recv, forward_send, forward_recv, chosen_sem, *blocks_of,
):
    leaf, middle = blocks_of[:per], blocks_of[per:]
    n = lax.axis_size("mode")
    group = n // per
    pair = 2
    peers = group // pair
    rounds = n // pair
    wide = pair * per
    m = lax.axis_index("mode")
    core = lax.axis_index("branch")
    h, g = m // group, lax.rem(m, group)
    line, side = g // pair, lax.rem(g, pair)
    across = pair * line + 1 - side
    blk, width = prod.shape[-2:]
    order = n * blk
    outer = lax.rem(line + h + 1, 2) == 1

    def remote(src, dst, send, recv, **device):
        return pltpu.make_async_remote_copy(
            src_ref=src,
            dst_ref=dst,
            send_sem=send,
            recv_sem=recv,
            device_id=device,
            device_id_type=MESH,
        )

    def column(line_at):
        return pair * line_at + side

    def up(k):
        return lax.rem(line + k, peers)

    def down(k):
        return lax.rem(line + peers - k, peers)

    def own_right_copy(q, e):
        return pltpu.make_async_copy(
            prod.at[0, :, e, pair * q + side], right.at[q, :, per * g + e], own_right.at[q, e]
        )

    def own_left_copy(q, e):
        return pltpu.make_async_copy(
            prod.at[1, :, e, pair * q + side], left.at[q, :, per * side + e], own_left.at[q, e]
        )

    def cross_right(q, e, source=None):
        return remote(
            prod.at[0, :, e, pair * q + 1 - side],
            right.at[q, :, per * (g if source is None else source) + e],
            cross_right_send.at[q, e],
            cross_right_recv.at[q, e],
            mode=h * group + across,
        )

    def cross_left(q, e, source=None):
        return remote(
            prod.at[1, :, e, pair * q + 1 - side],
            left.at[q, :, per * (side if source is None else source) + e],
            cross_left_send.at[q, e],
            cross_left_recv.at[q, e],
            mode=h * group + across,
        )

    def column_right(q, e, k, target, source):
        return remote(
            prod.at[0, :, e, pair * q + side],
            right.at[q, :, per * column(source) + e],
            column_send.at[q, e, k],
            column_recv.at[q, e, k],
            mode=h * group + column(target),
        )

    def relay_right(q, e, k, target, source):
        part = right.at[q, :, per * (pair * source + 1 - side) + e]
        return remote(
            part,
            part,
            relay_send.at[q, e, k],
            relay_recv.at[q, e, k],
            mode=h * group + column(target),
        )

    def entry(q):
        return wide * q // n

    def row_of(q, h_from, side_from):
        return lax.rem(wide * q + per * side_from + h_from, n)

    def deliver(q, i):
        return remote(
            result.at[q, :, i],
            middle[entry(q)].at[core, :, row_of(q, h, side)],
            deliver_send.at[q, i],
            deliver_recv.at[q, pair * h + side],
            mode=wide * line + i,
        )

    def deliver_own(q, i):
        return pltpu.make_async_copy(
            result.at[q, :, i],
            middle[entry(q)].at[core, :, row_of(q, h, side)],
            deliver_recv.at[q, pair * h + side],
        )

    def delivered(q, h_from, side_from):
        part = middle[entry(q)].at[core, :, row_of(q, h_from, side_from)]
        return pltpu.make_async_copy(part, part, deliver_recv.at[q, pair * h_from + side_from])

    def forward(q, h_from, side_from, owner):
        part = middle[entry(q)].at[owner, :, row_of(q, h_from, side_from)]
        at = pair * h_from + side_from
        return remote(
            part, part, forward_send.at[q, at], forward_recv.at[q, at], branch=1 - core
        )

    def leaf_copy(e):
        return pltpu.make_async_copy(leaves_ref.at[:, :, e], leaf[e], leaf_sem.at[e])

    middle_order = order_ref[4 + core]
    tile = min(256, order)

    def first_tile(slot, e, step):
        which = 1 - middle_order if slot == 0 else middle_order
        flag = order_ref[2 * core + which]
        left_leaf = 2 * which + flag
        right_leaf = 2 * which + 1 - flag
        at = pl.ds(pl.multiple_of(step * tile, tile), tile)
        real_part, imag_part = complex_rows(
            leaf[e][left_leaf, 0, at, :],
            leaf[e][left_leaf, 1, at, :],
            leaf[e][right_leaf, 0],
            leaf[e][right_leaf, 1],
        )
        blocks = tile // blk
        shape = (blocks, blk, width)
        to = pl.ds(step * blocks, blocks)
        prod[slot, 0, e, to] = real_part.astype(prod.dtype).reshape(shape)
        prod[slot, 1, e, to] = imag_part.astype(prod.dtype).reshape(shape)

    def later_tiles(slot, e):
        @pl.loop(1, order // tile)
        def _(step):
            first_tile(slot, e, step)

    def send_cross_right(q):
        for e in range(per):
            cross_right(q, e).start()

    def send_cross_left(q):
        for e in range(per):
            cross_left(q, e).start()
            own_left_copy(q, e).start()

    def send_column(q, e):
        for k in range(1, peers):
            column_right(q, e, k, up(k), line).start()
        own_right_copy(q, e).start()

    def send_relay(q, e):
        cross_right(q, e, across).wait_recv()
        for k in range(1, peers):
            relay_right(q, e, k, up(k), line).start()

    def relay_round(q):
        for e in range(per):
            send_column(q, e)
        for e in range(per):
            send_relay(q, e)

    def send_result(q, i):
        here = wide * line + i == m

        @pl.when(jnp.logical_not(here))
        def _():
            deliver(q, i).start()

        @pl.when(here)
        def _():
            deliver_own(q, i).start()

    def near(q):
        near_pair = lax.rem(line + h + 1, 2)
        for t in range(pair):
            send_result(q, near_pair * (pair * h + t) + (1 - near_pair) * (pair * t + side))

    def far(q):
        near_pair = lax.rem(line + h + 1, 2)
        for t in range(pair):
            send_result(
                q,
                near_pair * (pair * (1 - h) + t) + (1 - near_pair) * (pair * t + 1 - side),
            )

    row_tile = wide * blk

    def join_round(q):
        for e in range(per):
            own_right_copy(q, e).wait()
            own_left_copy(q, e).wait()
            cross_left(q, e, 1 - side).wait_recv()
            for k in range(1, peers):
                column_right(q, e, k, down(k), down(k)).wait_recv()
                relay_right(q, e, k, down(k), down(k)).wait_recv()

        real_part, imag_part = complex_rows(
            left[q, 0].reshape(row_tile, width),
            left[q, 1].reshape(row_tile, width),
            right[q, 0].reshape(order, width),
            right[q, 1].reshape(order, width),
        )
        result[q, 0] = real_part.astype(result.dtype).reshape(wide, blk, width)
        result[q, 1] = imag_part.astype(result.dtype).reshape(wide, blk, width)

    def top_entry(b):
        rows, half = n // 2, order // 2
        last = order_ref[order_ref.shape[0] - 1]
        at = pl.ds(core * rows, rows)
        value = slices_ref[b]
        top_real, top_imag = complex_rows(
            middle[b][last, 0, at].reshape(half, width),
            middle[b][last, 1, at].reshape(half, width),
            middle[b][1 - last, 0].reshape(order, width),
            middle[b][1 - last, 1].reshape(order, width),
        )
        real_part, imag_part = complex_rows(
            top_real.astype(prod.dtype),
            top_imag.astype(prod.dtype),
            chosen[value, 0],
            chosen[value, 1],
        )
        out_ref[0, b] = real_part
        out_ref[1, b] = imag_part

    barrier = pltpu.get_barrier_semaphore()
    for k in range(1, n):
        pl.semaphore_signal(
            barrier, inc=1, device_id={"mode": lax.rem(m + k, n)}, device_id_type=MESH
        )
    pl.semaphore_signal(barrier, inc=1, device_id={"branch": 1 - core}, device_id_type=MESH)
    for e in range(per):
        leaf_copy(e).start()
    boundary_copy = pltpu.make_async_copy(boundary_ref, chosen, chosen_sem)

    for e in range(per):
        leaf_copy(e).wait()
        first_tile(0, e, 0)
        if e == 0:
            pl.semaphore_wait(barrier, n)
        cross_right(0, e).start()
        send_column(0, e)
    for e in range(per):
        first_tile(1, e, 0)
        cross_left(0, e).start()
        own_left_copy(0, e).start()
    boundary_copy.start()
    for e in range(per):
        send_relay(0, e)
        later_tiles(0, e)
    for q in range(1, min(3, rounds)):
        send_cross_right(q)
    for e in range(per):
        later_tiles(1, e)
    for q in range(1, rounds):
        send_cross_left(q)
        if q + 2 < rounds:
            send_cross_right(q + 2)

    join_round(0)
    near(0)
    far(0)
    for q in range(1, min(3, rounds)):
        relay_round(q)
    for q in range(1, rounds):
        join_round(q)
        near(q)
        far(q)
        if q + 2 < rounds:
            relay_round(q + 2)

    boundary_copy.wait()
    for b in range(per):
        mine = [q for q in range(rounds) if entry(q) == b]
        sources = [(h_from, side_from) for h_from in range(per) for side_from in range(pair)]
        for q in mine:
            for h_from, side_from in sources:
                delivered(q, h_from, side_from).wait()
                forward(q, h_from, side_from, core).start()
        for q in mine:
            for h_from, side_from in sources:
                forward(q, h_from, side_from, 1 - core).wait_recv()
        top_entry(b)

    for q in range(rounds):
        for e in range(per):
            cross_right(q, e).wait_send()
            cross_left(q, e).wait_send()
            for k in range(1, peers):
                column_right(q, e, k, up(k), line).wait_send()
                relay_right(q, e, k, up(k), line).wait_send()
        for i in range(wide):

            @pl.when(wide * line + i != m)
            def _():
                deliver(q, i).wait_send()

        for h_from in range(per):
            for side_from in range(pair):
                forward(q, h_from, side_from, core).wait_send()


def contract(leaves, join_order, slice_values, boundary):
    n = lax.axis_size("mode")
    count, _, per, order, width = leaves.shape
    blk = order // n
    rounds, peers, wide = n // 2, n // per // 2, 2 * per
    dma = pltpu.SemaphoreType.DMA
    dtype = leaves.dtype
    return pl.pallas_call(
        functools.partial(contract_kernel, per),
        out_shape=jax.ShapeDtypeStruct((2, per, order // 2, width), jnp.float32),
        in_specs=[
            pl.BlockSpec(memory_space=pltpu.SMEM),
            pl.BlockSpec(memory_space=pltpu.SMEM),
            pl.BlockSpec(memory_space=pl.ANY),
            pl.BlockSpec(memory_space=pl.ANY),
        ],
        out_specs=pl.BlockSpec(memory_space=pltpu.VMEM),
        scratch_shapes=[
            pltpu.VMEM((2, 2, per, n, blk, width), dtype),
            pltpu.VMEM((rounds, 2, n, blk, width), dtype),
            pltpu.VMEM((rounds, 2, wide, blk, width), dtype),
            pltpu.VMEM((rounds, 2, wide, blk, width), dtype),
            pltpu.VMEM(boundary.shape, dtype),
            dma((per,)),
            dma((rounds, per)),
            dma((rounds, per)),
            dma((rounds, per)),
            dma((rounds, per)),
            dma((rounds, per)),
            dma((rounds, per)),
            dma((rounds, per, peers)),
            dma((rounds, per, peers)),
            dma((rounds, per, peers)),
            dma((rounds, per, peers)),
            dma((rounds, wide)),
            dma((rounds, wide)),
            dma((rounds, wide)),
            dma((rounds, wide)),
            dma(()),
        ]
        + [pltpu.VMEM((count, 2, order, width), dtype)] * per
        + [pltpu.VMEM((2, 2, n, blk, width), dtype)] * per,
        compiler_params=pltpu.CompilerParams(
            collective_id=0, has_side_effects=True, vmem_limit_bytes=58 << 20
        ),
        name="contract",
    )(join_order, slice_values, leaves, boundary)


def per_device(leaves, join_order, slice_values, boundary):
    return contract(leaves, join_order, slice_values, boundary)


def solution(mesh):
    in_specs = (P("branch", None, ("cuts", "mode"), None, None), P(), P(("cuts", "mode")), P())
    out_specs = P(None, ("cuts", "mode"), "branch", None)
    return jax.shard_map(
        per_device, mesh=mesh, in_specs=in_specs, out_specs=out_specs, check_vma=False
    )
```

time: 92 us -> 90.7 us (0.986)
  Pallas kernels: 91.3 us -> 86.2 us
  local copies, waits for them, and re-layouts: 0 us -> 3.08 us
    pallas_call x2 -> x1, Pallas kernels: 91.3 us -> 86.2 us  [contract(): pl.pallas_call(functools.partial(contract_kernel, per), out_shape=jax.Sha...]
    unnamed x0 -> x1, local copies, waits for them, and re-layouts: none -> 3.08 us
where the time goes in v1:
time: 90.7 us; the launch traced here: 89.3 us
  Pallas kernels  86.2 us (95%)
  local copies, waits for them, and re-layouts  3.08 us (3%)
    pallas_call x1, Pallas kernels, contract(): pl.pallas_call(functools.partial(contract_kernel, per), out_shape=jax.Sha...  86.2 us
    unnamed x1, local copies, waits for them, and re-layouts  3.08 us

profile of v1, /device:TPU:11, one launch (start us, length us, event | category | flops | bytes accessed | tf_op | source)
XLA Modules:
  0.0 89.3 jit_solution(8684328943591314744)
XLA Ops:
  0.0 86.2 %contract.1 = f32[2,2,256,512]{3,2,1,0:T(8,128)} custom-call(s32[7]{0:T(128)} %order_ref.1, s32[2]{0:T(128)} %slices_ref.1, bf16[4,2,2,512,512]{4,3,2,1,0:T(8,128)(2,1)} %leaves_ref.1, bf16[2,2,512,512]{3,2,1,0:T(8,128)(2,1)} %boundary_ref.1), custom_call_target="tpu_custom_call" | custom-call | tf_op jit(solution)/shard_map/contract/pallas_call | solution.py:348
  86.2 3.1 %copy.6 = f32[2,2,256,512]{3,2,1,0:T(8,128)} copy(f32[2,2,256,512]{3,2,1,0:T(8,128)} %contract.1) | data formatting | bytes 4194304

commit v2 on v1

--- a/solution.py
+++ b/solution.py
@@ -20,13 +20,26 @@
     return real_part, imag_part
 
 
+OUTER = (("C", -2), ("Xb", 2), ("R", -7), ("Oa", 1), ("Y", -2), ("Ob", 2), ("Xa", 1), ("L", -3))
+INNER = (("Xb", 3), ("Oa", 1), ("Xa", 2), ("R", -2), ("Ob", 2), ("Y", 0), ("L", -2), ("C", -3))
+
+
+def schedule(lags, rounds):
+    steps = [[] for _ in range(2 * rounds + 1)]
+    for move, lag in lags:
+        for q in range(1 if move in "RLCY" else 0, rounds):
+            steps[min(max(2 * q + lag, 0), 2 * rounds)].append((move, q))
+    return steps
+
+
 def contract_kernel(
     per, order_ref, slices_ref, leaves_ref, boundary_ref, out_ref,
     prod, right, left, result, chosen,
-    leaf_sem, own_right, own_left,
+    leaf_sem, own_right,
     cross_right_send, cross_right_recv, cross_left_send, cross_left_recv,
     column_send, column_recv, relay_send, relay_recv,
-    deliver_send, deliver_recv, forward_send, forward_recv, chosen_sem, *blocks_of,
+    deliver_send, deliver_recv,
+    forward_send, forward_recv, chosen_sem, *blocks_of,
 ):
     leaf, middle = blocks_of[:per], blocks_of[per:]
     n = lax.axis_size("mode")
@@ -68,11 +81,6 @@
             prod.at[0, :, e, pair * q + side], right.at[q, :, per * g + e], own_right.at[q, e]
         )
 
-    def own_left_copy(q, e):
-        return pltpu.make_async_copy(
-            prod.at[1, :, e, pair * q + side], left.at[q, :, per * side + e], own_left.at[q, e]
-        )
-
     def cross_right(q, e, source=None):
         return remote(
             prod.at[0, :, e, pair * q + 1 - side],
@@ -82,10 +90,10 @@
             mode=h * group + across,
         )
 
-    def cross_left(q, e, source=None):
+    def cross_left(q, e):
         return remote(
             prod.at[1, :, e, pair * q + 1 - side],
-            left.at[q, :, per * (side if source is None else source) + e],
+            left.at[q, :, e],
             cross_left_send.at[q, e],
             cross_left_recv.at[q, e],
             mode=h * group + across,
@@ -116,6 +124,12 @@
     def row_of(q, h_from, side_from):
         return lax.rem(wide * q + per * side_from + h_from, n)
 
+    def straight(origin, t):
+        return per * origin + pair * t + side
+
+    def crossing(origin, t):
+        return per * origin + pair * t + 1 - side
+
     def deliver(q, i):
         return remote(
             result.at[q, :, i],
@@ -147,7 +161,7 @@
         return pltpu.make_async_copy(leaves_ref.at[:, :, e], leaf[e], leaf_sem.at[e])
 
     middle_order = order_ref[4 + core]
-    tile = min(256, order)
+    tile = min(128, order)
 
     def first_tile(slot, e, step):
         which = 1 - middle_order if slot == 0 else middle_order
@@ -179,67 +193,65 @@
     def send_cross_left(q):
         for e in range(per):
             cross_left(q, e).start()
-            own_left_copy(q, e).start()
-
-    def send_column(q, e):
-        for k in range(1, peers):
-            column_right(q, e, k, up(k), line).start()
-        own_right_copy(q, e).start()
+
+    def send_column(q):
+        for e in range(per):
+            for k in range(1, peers):
+                column_right(q, e, k, up(k), line).start()
+            own_right_copy(q, e).start()
 
     def send_relay(q, e):
         cross_right(q, e, across).wait_recv()
         for k in range(1, peers):
             relay_right(q, e, k, up(k), line).start()
 
-    def relay_round(q):
-        for e in range(per):
-            send_column(q, e)
+    def send_relays(q):
         for e in range(per):
             send_relay(q, e)
 
-    def send_result(q, i):
-        here = wide * line + i == m
-
-        @pl.when(jnp.logical_not(here))
-        def _():
-            deliver(q, i).start()
-
-        @pl.when(here)
-        def _():
-            deliver_own(q, i).start()
-
-    def near(q):
-        near_pair = lax.rem(line + h + 1, 2)
-        for t in range(pair):
-            send_result(q, near_pair * (pair * h + t) + (1 - near_pair) * (pair * t + side))
-
-    def far(q):
-        near_pair = lax.rem(line + h + 1, 2)
-        for t in range(pair):
-            send_result(
-                q,
-                near_pair * (pair * (1 - h) + t) + (1 - near_pair) * (pair * t + 1 - side),
-            )
-
-    row_tile = wide * blk
-
-    def join_round(q):
+    def send_straight(q, origin):
+        for t in range(per // pair):
+            i = straight(origin, t)
+            here = wide * line + i == m
+
+            @pl.when(jnp.logical_not(here))
+            def _():
+                deliver(q, i).start()
+
+            @pl.when(here)
+            def _():
+                deliver_own(q, i).start()
+
+    def send_crossing(q, origin):
+        for t in range(per // pair):
+            deliver(q, crossing(origin, t)).start()
+
+    rows_of = per * blk
+
+    def second_join(q, origin, left_real, left_imag):
+        real_part, imag_part = complex_rows(
+            left_real.reshape(rows_of, width),
+            left_imag.reshape(rows_of, width),
+            right[q, 0].reshape(order, width),
+            right[q, 1].reshape(order, width),
+        )
+        to = pl.ds(per * origin, per)
+        result[q, 0, to] = real_part.astype(result.dtype).reshape(per, blk, width)
+        result[q, 1, to] = imag_part.astype(result.dtype).reshape(per, blk, width)
+
+    def join_own(q):
         for e in range(per):
             own_right_copy(q, e).wait()
-            own_left_copy(q, e).wait()
-            cross_left(q, e, 1 - side).wait_recv()
             for k in range(1, peers):
                 column_right(q, e, k, down(k), down(k)).wait_recv()
                 relay_right(q, e, k, down(k), down(k)).wait_recv()
-
-        real_part, imag_part = complex_rows(
-            left[q, 0].reshape(row_tile, width),
-            left[q, 1].reshape(row_tile, width),
-            right[q, 0].reshape(order, width),
-            right[q, 1].reshape(order, width),
-        )
-        result[q, 0] = real_part.astype(result.dtype).reshape(wide, blk, width)
-        result[q, 1] = imag_part.astype(result.dtype).reshape(wide, blk, width)
+        at = pair * q + side
+        second_join(q, side, prod[1, 0, :, at], prod[1, 1, :, at])
+
+    def join_across(q):
+        for e in range(per):
+            cross_left(q, e).wait_recv()
+        second_join(q, 1 - side, left[q, 0], left[q, 1])
 
     def top_entry(b):
         rows, half = n // 2, order // 2
@@ -261,15 +273,15 @@
         out_ref[0, b] = real_part
         out_ref[1, b] = imag_part
 
+    boundary_copy = pltpu.make_async_copy(boundary_ref, chosen, chosen_sem)
+    for e in range(per):
+        leaf_copy(e).start()
     barrier = pltpu.get_barrier_semaphore()
     for k in range(1, n):
         pl.semaphore_signal(
             barrier, inc=1, device_id={"mode": lax.rem(m + k, n)}, device_id_type=MESH
         )
     pl.semaphore_signal(barrier, inc=1, device_id={"branch": 1 - core}, device_id_type=MESH)
-    for e in range(per):
-        leaf_copy(e).start()
-    boundary_copy = pltpu.make_async_copy(boundary_ref, chosen, chosen_sem)
 
     for e in range(per):
         leaf_copy(e).wait()
@@ -277,35 +289,50 @@
         if e == 0:
             pl.semaphore_wait(barrier, n)
         cross_right(0, e).start()
-        send_column(0, e)
+        for k in range(1, peers):
+            column_right(0, e, k, up(k), line).start()
+        own_right_copy(0, e).start()
     for e in range(per):
         first_tile(1, e, 0)
         cross_left(0, e).start()
-        own_left_copy(0, e).start()
     boundary_copy.start()
     for e in range(per):
         send_relay(0, e)
         later_tiles(0, e)
-    for q in range(1, min(3, rounds)):
-        send_cross_right(q)
     for e in range(per):
         later_tiles(1, e)
-    for q in range(1, rounds):
-        send_cross_left(q)
-        if q + 2 < rounds:
-            send_cross_right(q + 2)
-
-    join_round(0)
-    near(0)
-    far(0)
-    for q in range(1, min(3, rounds)):
-        relay_round(q)
-    for q in range(1, rounds):
-        join_round(q)
-        near(q)
-        far(q)
-        if q + 2 < rounds:
-            relay_round(q + 2)
+
+    moves = {
+        "R": send_cross_right,
+        "L": send_cross_left,
+        "C": send_column,
+        "Y": send_relays,
+        "Oa": lambda q: send_straight(q, side),
+        "Ob": lambda q: send_straight(q, 1 - side),
+        "Xa": lambda q: send_crossing(q, side),
+        "Xb": lambda q: send_crossing(q, 1 - side),
+    }
+
+    def run(steps):
+        for move, q in steps:
+            moves[move](q)
+
+    outer_steps, inner_steps = schedule(OUTER, rounds), schedule(INNER, rounds)
+    for step in range(2 * rounds + 1):
+        if outer_steps[step] == inner_steps[step]:
+            run(outer_steps[step])
+        else:
+
+            @pl.when(outer)
+            def _():
+                run(outer_steps[step])
+
+            @pl.when(jnp.logical_not(outer))
+            def _():
+                run(inner_steps[step])
+
+        if step < 2 * rounds:
+            (join_across if step % 2 else join_own)(step // 2)
 
     boundary_copy.wait()
     for b in range(per):
@@ -351,18 +378,17 @@
         in_specs=[
             pl.BlockSpec(memory_space=pltpu.SMEM),
             pl.BlockSpec(memory_space=pltpu.SMEM),
-            pl.BlockSpec(memory_space=pl.ANY),
-            pl.BlockSpec(memory_space=pl.ANY),
+            pl.BlockSpec(memory_space=pltpu.HBM),
+            pl.BlockSpec(memory_space=pltpu.HBM),
         ],
         out_specs=pl.BlockSpec(memory_space=pltpu.VMEM),
         scratch_shapes=[
             pltpu.VMEM((2, 2, per, n, blk, width), dtype),
             pltpu.VMEM((rounds, 2, n, blk, width), dtype),
-            pltpu.VMEM((rounds, 2, wide, blk, width), dtype),
+            pltpu.VMEM((rounds, 2, per, blk, width), dtype),
             pltpu.VMEM((rounds, 2, wide, blk, width), dtype),
             pltpu.VMEM(boundary.shape, dtype),
             dma((per,)),
-            dma((rounds, per)),
             dma((rounds, per)),
             dma((rounds, per)),
             dma((rounds, per)),
@@ -381,10 +407,15 @@
         + [pltpu.VMEM((count, 2, order, width), dtype)] * per
         + [pltpu.VMEM((2, 2, n, blk, width), dtype)] * per,
         compiler_params=pltpu.CompilerParams(
-            collective_id=0, has_side_effects=True, vmem_limit_bytes=58 << 20
+            collective_id=0, has_side_effects=True, vmem_limit_bytes=48 << 20
         ),
         name="contract",
-    )(join_order, slice_values, leaves, boundary)
+    )(
+        pltpu.with_memory_space_constraint(join_order, pltpu.HBM),
+        pltpu.with_memory_space_constraint(slice_values, pltpu.HBM),
+        pltpu.with_memory_space_constraint(leaves, pltpu.HBM),
+        pltpu.with_memory_space_constraint(boundary, pltpu.HBM),
+    )
 
 
 def per_device(leaves, join_order, slice_values, boundary):

time: 90.7 us -> 83.8 us (0.924); the launches traced: 89.3 us -> 83.5 us
  Pallas kernels: 86.2 us -> 82.2 us
  local copies, waits for them, and re-layouts: 3.08 us -> 1.32 us
    pallas_call x1, Pallas kernels: 86.2 us -> 82.2 us  [contract(): pl.pallas_call(functools.partial(contract_kernel, per), out_shape=jax.Sha...]
    unnamed x1, local copies, waits for them, and re-layouts: 3.08 us -> 1.32 us
where the time goes in v2:
time: 83.8 us; the launch traced here: 83.5 us
  Pallas kernels  82.2 us (98%)
  local copies, waits for them, and re-layouts  1.32 us (2%)
    pallas_call x1, Pallas kernels, contract(): pl.pallas_call(functools.partial(contract_kernel, per), out_shape=jax.Sha...  82.2 us

profile of v2, /device:TPU:11, one launch (start us, length us, event | category | flops | bytes accessed | tf_op | source)
XLA Modules:
  0.0 83.5 jit_solution(8438508309560404402)
XLA Ops:
  0.0 82.2 %contract.1 = f32[2,2,256,512]{3,2,1,0:T(8,128)S(1)} custom-call(s32[7]{0:T(128)} %order_ref.1, s32[2]{0:T(128)} %slices_ref.1, bf16[4,2,2,512,512]{4,3,2,1,0:T(8,128)(2,1)} %leaves_ref.1, bf16[2,2,512,512]{3,2,1,0:T(8,128)(2,1)} %boundary_ref.1), custom_call_target="tpu_custom_call" | custom-call | tf_op jit(solution)/shard_map/contract/pallas_call | solution.py:375
  82.2 1.3 %copy.6 = f32[2,2,256,512]{3,2,1,0:T(8,128)} copy(f32[2,2,256,512]{3,2,1,0:T(8,128)S(1)} %contract.1) | data formatting | bytes 4194304

commit v3 on v2

--- a/solution.py
+++ b/solution.py
@@ -335,17 +335,26 @@
             (join_across if step % 2 else join_own)(step // 2)
 
     boundary_copy.wait()
+    sources = [(h_from, side_from) for h_from in range(per) for side_from in range(pair)]
+
+    def share(q):
+        for h_from, side_from in sources:
+            delivered(q, h_from, side_from).wait()
+            forward(q, h_from, side_from, core).start()
+
+    mine = [[q for q in range(rounds) if entry(q) == b] for b in range(per)]
+    for q in mine[0]:
+        share(q)
     for b in range(per):
-        mine = [q for q in range(rounds) if entry(q) == b]
-        sources = [(h_from, side_from) for h_from in range(per) for side_from in range(pair)]
-        for q in mine:
-            for h_from, side_from in sources:
-                delivered(q, h_from, side_from).wait()
-                forward(q, h_from, side_from, core).start()
-        for q in mine:
+        for q in mine[b]:
             for h_from, side_from in sources:
                 forward(q, h_from, side_from, 1 - core).wait_recv()
+        later = mine[b + 1] if b + 1 < per else []
+        for q in later[:-1]:
+            share(q)
         top_entry(b)
+        for q in later[-1:]:
+            share(q)
 
     for q in range(rounds):
         for e in range(per):

time: 83.8 us -> 83.7 us (level)
  no operation moved by 1% of the time
where the time goes in v3:
time: 83.7 us; the launch traced here: 83.5 us
  Pallas kernels  82.2 us (98%)
  local copies, waits for them, and re-layouts  1.32 us (2%)
    pallas_call x1, Pallas kernels, contract(): pl.pallas_call(functools.partial(contract_kernel, per), out_shape=jax.Sha...  82.2 us

profile of v3, /device:TPU:11, one launch (start us, length us, event | category | flops | bytes accessed | tf_op | source)
XLA Modules:
  0.0 83.5 jit_solution(1297378974654378258)
XLA Ops:
  0.0 82.2 %contract.1 = f32[2,2,256,512]{3,2,1,0:T(8,128)S(1)} custom-call(s32[7]{0:T(128)} %order_ref.1, s32[2]{0:T(128)} %slices_ref.1, bf16[4,2,2,512,512]{4,3,2,1,0:T(8,128)(2,1)} %leaves_ref.1, bf16[2,2,512,512]{3,2,1,0:T(8,128)(2,1)} %boundary_ref.1), custom_call_target="tpu_custom_call" | custom-call | tf_op jit(solution)/shard_map/contract/pallas_call | solution.py:384
  82.2 1.3 %copy.6 = f32[2,2,256,512]{3,2,1,0:T(8,128)} copy(f32[2,2,256,512]{3,2,1,0:T(8,128)S(1)} %contract.1) | data formatting | bytes 4194304
